TPU v7x, 32 devices: a whole 2x2x4 slice. The times are simulated.
32 devices in a mesh: aper: 8 (over y, x, core), swath: 4 (over z).
Axes of the slice: x: 2, y: 2, z: 4, core: 2. Of those that a mesh axis runs over, the one named last changes fastest.
Arguments:
- polar_field: float32 [2, 1024, 4096], P(None, 'aper', 'swath'), may hold values from -6 to 6
- tap_index: int32 [3, 8, 2, 8, 128], P(None, 'aper'), may hold values from 0 to 127
- tap_weight: float32 [3, 8, 2, 8, 128], P(None, 'aper'), may hold values from -1.5 to 1.5
- range_shift: float32 [3, 8, 2, 128], P(None, 'aper'), may hold values from -8 to 8
- range_gain: float32 [3, 4096], P(None, 'swath'), may hold values from 0.1 to 1.9
- tile_owner: int32 [8, 4, 8, 1], P('aper', 'swath'), may hold values from 0 to 7; in each aligned block of 8 rows (0 to 7, 8 to 15, ..., all dimensions but the last counted through in order) at most 2 rows name the same one
- block_weights: float32 [8, 4, 8, 128, 128], P('aper', 'swath'), may hold values from -0.5 to 0.5
- kernel_index: int32 [8, 4], P('aper', 'swath'), may hold values from 0 to 15
- kernel_bank: float32 [16, 81], replicated, may hold values from -0.625 to 0.625
Outputs:
- deconvolved: float32 [2, 1024, 512], P(None, 'aper', 'swath')
Inputs may be any that keep to these rules, and one draw needn't show every extreme that they name: `tile_owner`: the 8 polar blocks of one device name any one owner at most 2 times, and some device names one owner exactly 2 times; every owner is named somewhere.
All inputs are finite; a program needn't handle non-finite values.
Results may differ from a plain program's by a relative error of at most 0.00011.
Values sent between devices are 32-bit elements; how exact they have to be, the bound alone decides.
A program may use at most 128 MiB of HBM per device.

v0:
```python
import functools
import math

import jax
import jax.numpy as jnp
import numpy as np
from jax import lax
from jax.experimental import pallas as pl
from jax.experimental.pallas import tpu as pltpu
from jax.sharding import PartitionSpec as P

ANGLES = 128
RANGE_BINS = 1024
LANES = 128
GROUPS = RANGE_BINS // LANES
WIDE = 2 * LANES
TILE_ROWS = 128
TAPS = 8
CHUNKS = 4
ROWS = ANGLES // CHUNKS
EDGE = 8
REACH = 4
MESH = pl.DeviceIdType.MESH
F32 = jnp.float32
BF16 = jnp.bfloat16


def split(value):
    high = value.astype(BF16)
    return high, (value - high.astype(F32)).astype(BF16)


def product(left, right):
    def dot(a, b):
        return jnp.dot(a, b, preferred_element_type=F32)

    return dot(left[0], right[0]) + dot(left[1], right[0]) + dot(left[0], right[1])


def turn(value):
    half = (value - jnp.floor(value + 0.5)) * F32(math.pi)
    square = half * half
    sine = F32(-1.0 / math.factorial(15))
    for order in (13, 11, 9, 7, 5, 3, 1):
        sign = 1.0 if order % 4 == 1 else -1.0
        sine = sine * square + F32(sign / math.factorial(order))
    sine = sine * half
    cosine = F32(1.0 / math.factorial(16))
    for order in (14, 12, 10, 8, 6, 4, 2, 0):
        sign = 1.0 if order % 4 == 0 else -1.0
        cosine = cosine * square + F32(sign / math.factorial(order))
    return 1.0 - 2.0 * sine * sine, 2.0 * sine * cosine


def four(x):
    (ar, ai), (br, bi), (cr, ci), (dr, di) = x
    sr, si, tr, ti = ar + cr, ai + ci, ar - cr, ai - ci
    ur, ui, vr, vi = br + dr, bi + di, br - dr, bi - di
    return [(sr + ur, si + ui), (tr + vi, ti - vr), (sr - ur, si - ui), (tr - vi, ti + vr)]


def eight(x):
    even, odd = four(x[0::2]), four(x[1::2])
    root = F32(math.sqrt(0.5))
    turned = [
        odd[0],
        ((odd[1][0] + odd[1][1]) * root, (odd[1][1] - odd[1][0]) * root),
        (odd[2][1], -odd[2][0]),
        ((odd[3][1] - odd[3][0]) * root, -(odd[3][0] + odd[3][1]) * root),
    ]
    first = [(e[0] + o[0], e[1] + o[1]) for e, o in zip(even, turned)]
    return first + [(e[0] - o[0], e[1] - o[1]) for e, o in zip(even, turned)]


def twiddle(pairs, cos_ref, sin_ref):
    out = [pairs[0]]
    for group in range(1, GROUPS):
        a, b = pairs[group]
        c, s = cos_ref[group : group + 1, :], sin_ref[group : group + 1, :]
        out.append((a * c + b * s, b * c - a * s))
    return out


def short_dft(pairs, table):
    rows = pairs[0][0].shape[0]
    stacked = jnp.concatenate([jnp.concatenate(pair, axis=1) for pair in pairs], axis=0)
    out = product(split(stacked), table)
    return [out[g * rows : (g + 1) * rows] for g in range(len(pairs))]


def forward(pairs, table, cos_ref, sin_ref):
    return short_dft(twiddle(eight(pairs), cos_ref, sin_ref), table)


def inverse(merged, table, cos_ref, sin_ref, gain):
    out = short_dft([(im, re) for re, im in merged], table)
    pairs = eight(twiddle([(o[:, :LANES], o[:, LANES:]) for o in out], cos_ref, sin_ref))
    scaled = gain * F32(1.0 / RANGE_BINS)
    result = []
    for group, (im, re) in enumerate(pairs):
        weight = scaled[:, group * LANES : (group + 1) * LANES]
        result.append((re * weight, im * weight))
    return result


def kernel(
    peers,
    swaths,
    sections,
    polar,
    taps,
    weights,
    shifts,
    gains,
    owner,
    block_weights,
    kernel_index,
    bank,
    table_high,
    table_low,
    cos_ref,
    sin_ref,
    result,
    matrix,
    phases,
    spec0,
    spec1,
    spec2,
    got0,
    got1,
    got2,
    mixed,
    total,
    image,
    mat_send,
    mat_got,
    part,
    part_got,
    row_halo,
    col_halo,
    flipped,
    shifted,
    send_sem,
    recv_sem,
    mat_sem,
    part_send,
    part_recv,
    halo_send,
    halo_recv,
):
    me = lax.axis_index("aper")
    column = lax.axis_index("swath")
    levels = peers.bit_length() - 1

    row_halo[...] = jnp.zeros_like(row_halo)
    col_halo[...] = jnp.zeros_like(col_halo)

    around = [(da, ds) for da in (-1, 0, 1) for ds in (-1, 0, 1) if (da, ds) != (0, 0)]
    barrier = pltpu.get_barrier_semaphore()
    for level in range(levels):
        pl.semaphore_signal(
            barrier, inc=1, device_id=(me ^ (1 << level), column), device_id_type=MESH
        )
    for da, ds in around:
        where = (lax.rem(me + da + peers, peers), lax.rem(column + ds + swaths, swaths))
        pl.semaphore_signal(barrier, inc=1, device_id=where, device_id_type=MESH)

    bits = [lax.rem(me // (1 << step), 2) for step in range(levels)]
    table = (table_high[...], table_low[...])

    def interp(step, child):
        index = taps[step, 0, child]
        weight = weights[step, 0, child]
        rows = lax.broadcasted_iota(jnp.int32, (ANGLES, ANGLES), 0)
        built = jnp.zeros((ANGLES, ANGLES), F32)
        for tap in range(TAPS):
            built = built + jnp.where(
                index[tap : tap + 1, :] == rows, weight[tap : tap + 1, :], F32(0.0)
            )
        return built.T

    def fill_phases(step, side, child):
        row = shifts[step, 0, pl.ds(child, 1), :]
        shift = jnp.broadcast_to(row, (ANGLES, LANES)).T
        lane = lax.broadcasted_iota(jnp.int32, (ANGLES, LANES), 1)
        signed = jnp.where(lane < LANES // 2, lane, lane - LANES).astype(F32)
        unit = shift * F32(-1.0 / RANGE_BINS)
        step_cos, step_sin = turn(unit)
        a, b = turn(unit * (signed * F32(GROUPS)))
        for group in range(GROUPS):
            phases[step, side, group, 0] = a
            phases[step, side, group, 1] = b
            if group + 1 < GROUPS:
                a, b = a * step_cos - b * step_sin, b * step_cos + a * step_sin

    def steered(step, side, group, rows, value):
        a = phases[step, side, group, 0, rows, :]
        b = phases[step, side, group, 1, rows, :]
        re, im = value[:, :LANES], value[:, LANES:]
        return jnp.concatenate([a * re - b * im, b * re + a * im], axis=1)

    def lanes(group):
        return slice(group * WIDE, (group + 1) * WIDE)

    def chunk(k):
        return slice(k * ROWS, (k + 1) * ROWS)

    def exchange(step, k, source, target):
        return pltpu.make_async_remote_copy(
            src_ref=source.at[pl.ds(k * ROWS, ROWS)],
            dst_ref=target.at[pl.ds(k * ROWS, ROWS)],
            send_sem=send_sem.at[step, k],
            recv_sem=recv_sem.at[step, k],
            device_id=(me ^ (1 << step), column),
            device_id_type=MESH,
        )

    def store_wide(target, rows, values):
        for group in range(GROUPS):
            target[rows, lanes(group)] = values[group]

    def merged_rows(rows):
        pairs = []
        for group in range(GROUPS):
            value = total[rows, lanes(group)]
            pairs.append((value[:, :LANES], value[:, LANES:]))
        return pairs

    everything = slice(0, ANGLES)

    copies0 = []
    for k in range(CHUNKS):
        rows = chunk(k)
        pairs = [
            (polar[0, rows, g * LANES : (g + 1) * LANES], polar[1, rows, g * LANES : (g + 1) * LANES])
            for g in range(GROUPS)
        ]
        store_wide(spec0, rows, forward(pairs, table, cos_ref, sin_ref))
        if k == 0:
            pl.semaphore_wait(barrier, levels + len(around))
        copies0.append(exchange(0, k, spec0, got0))
        copies0[-1].start()
    mat_send[...] = interp(1, 1 - bits[1])
    mat_copy = pltpu.make_async_remote_copy(
        src_ref=mat_send,
        dst_ref=mat_got,
        send_sem=mat_sem.at[0],
        recv_sem=mat_sem.at[1],
        device_id=(me ^ 2, column),
        device_id_type=MESH,
    )
    mat_copy.start()
    fill_phases(0, 0, bits[0])
    fill_phases(0, 1, 1 - bits[0])

    def mix(step, side, source, first):
        left = split(interp(step, bits[step] if side == 0 else 1 - bits[step]))
        for group in range(GROUPS):
            value = product(left, split(source[:, lanes(group)]))
            value = steered(step, side, group, everything, value)
            if not first:
                value = value + total[:, lanes(group)]
            total[:, lanes(group)] = value

    mix(0, 0, spec0, True)
    for copy in copies0:
        copy.wait()
    mix(0, 1, got0, False)
    for k in range(CHUNKS):
        rows = chunk(k)
        pairs = inverse(merged_rows(rows), table, cos_ref, sin_ref, gains[0:1, :])
        store_wide(spec1, rows, forward(pairs, table, cos_ref, sin_ref))

    mat_copy.wait()
    copies1 = []
    for k in range(CHUNKS):
        rows = chunk(k)
        left = split(mat_got[rows, :])
        for group in range(GROUPS):
            mixed[rows, lanes(group)] = product(left, split(spec1[:, lanes(group)]))
        copies1.append(exchange(1, k, mixed, got1))
        copies1[-1].start()
    fill_phases(1, 0, bits[1])
    fill_phases(1, 1, 1 - bits[1])
    mix(1, 0, spec1, True)
    copies2 = []
    for k in range(CHUNKS):
        rows = chunk(k)
        copies1[k].wait()
        pairs = []
        for group in range(GROUPS):
            value = total[rows, lanes(group)] + steered(
                1, 1, group, rows, got1[rows, lanes(group)]
            )
            pairs.append((value[:, :LANES], value[:, LANES:]))
        pairs = inverse(pairs, table, cos_ref, sin_ref, gains[1:2, :])
        store_wide(spec2, rows, forward(pairs, table, cos_ref, sin_ref))
        copies2.append(exchange(2, k, spec2, got2))
        copies2[-1].start()
        if k == 0:
            fill_phases(2, 0, bits[2])
            fill_phases(2, 1, 1 - bits[2])

    mix(2, 0, spec2, True)
    for copy in copies2:
        copy.wait()
    mix(2, 1, got2, False)
    for k in range(CHUNKS):
        rows = chunk(k)
        pairs = inverse(merged_rows(rows), table, cos_ref, sin_ref, gains[2:3, :])
        store_wide(image, rows, [jnp.concatenate(pair, axis=1) for pair in pairs])

    for q in range(GROUPS):
        matrix[q] = product(split(block_weights[0, 0, q]), split(image[:, lanes(q)]))

    def gathered(d):
        value = None
        for q in range(GROUPS):
            hit = jnp.where(owner[q] == d, F32(1.0), F32(0.0))
            value = hit * matrix[q] if value is None else value + hit * matrix[q]
        return value

    def part_copy(level, slot, source, target):
        return pltpu.make_async_remote_copy(
            src_ref=source,
            dst_ref=target,
            send_sem=part_send.at[slot],
            recv_sem=part_recv.at[slot],
            device_id=(me ^ (1 << level), column),
            device_id_type=MESH,
        )

    half = peers // 2
    copies = []
    for d in range(half):
        part[half + d] = gathered(2 * d + 1 - bits[0])
        copies.append(part_copy(0, d, part.at[half + d], part_got.at[d]))
        copies[-1].start()
    for d in range(half):
        part[d] = gathered(2 * d + bits[0])
    for d in range(half):
        copies[d].wait()
        part[d] = part[d] + part_got[d]
    base, here = half, 0
    count = half
    for level in range(1, levels):
        count = count // 2
        copies = []
        for d in range(count):
            copies.append(
                part_copy(
                    level,
                    base + d,
                    part.at[here + 2 * d + 1 - bits[level]],
                    part_got.at[base + d],
                )
            )
            copies[-1].start()
        after = peers + base - half
        for d in range(count):
            copies[d].wait()
            part[after + d] = part[here + 2 * d + bits[level]] + part_got[base + d]
        here = after
        base = base + count
    tile = part.at[here]

    for plane in range(2):
        flipped[plane] = tile[:, plane * LANES : (plane + 1) * LANES].T

    def halo_copy(da, ds):
        slot = [r for r in range(len(around)) if around[r] == (-da, -ds)][0]
        if da != 0:
            edge = 0 if da < 0 else TILE_ROWS - EDGE
            source = tile.at[pl.ds(edge, EDGE)]
            target = row_halo.at[1 if da < 0 else 0, 1 - ds]
        else:
            edge = 0 if ds < 0 else LANES - EDGE
            source = flipped.at[:, pl.ds(edge, EDGE)]
            target = col_halo.at[1 if ds < 0 else 0]
        return pltpu.make_async_remote_copy(
            src_ref=source,
            dst_ref=target,
            send_sem=halo_send.at[slot],
            recv_sem=halo_recv.at[slot],
            device_id=(me + da, column + ds),
            device_id_type=MESH,
        )

    def present(da, ds):
        found = None
        for place, step, extent in ((me, da, peers), (column, ds, swaths)):
            if step != 0:
                inside = place > 0 if step < 0 else place < extent - 1
                found = inside if found is None else jnp.logical_and(found, inside)
        return found

    for da, ds in around:

        @pl.when(present(da, ds))
        def _(da=da, ds=ds):
            halo_copy(da, ds).start()

    for da, ds in around:

        @pl.when(present(da, ds))
        def _(da=da, ds=ds):
            halo_copy(da, ds).wait_send()
            halo_copy(-da, -ds).wait_recv()

    lane = lax.broadcasted_iota(jnp.int32, (EDGE, LANES), 1)
    chosen = kernel_index[0]
    gap = jnp.zeros((LANES - 2 * EDGE, LANES), F32)
    for plane in range(2):
        cut = slice(plane * LANES, (plane + 1) * LANES)

        def strip(end):
            side = jnp.where(
                lane < LANES // 2, row_halo[end, 2, :, cut], row_halo[end, 0, :, cut]
            )
            return jnp.concatenate([row_halo[end, 1, :, cut], side], axis=1)

        side = jnp.concatenate([col_halo[1, plane], gap, col_halo[0, plane]], axis=0).T
        middle = jnp.concatenate([tile[:, cut], side], axis=1)
        whole = jnp.concatenate([strip(0), middle, strip(1)], axis=0)
        summed = jnp.zeros((TILE_ROWS, LANES), F32)
        for v in range(2 * REACH + 1):
            moved = whole if v == REACH else pltpu.roll(whole, (REACH - v) % WIDE, 1)
            shifted[v] = moved[:, :LANES]
            for u in range(2 * REACH + 1):
                start = EDGE - REACH + u
                summed = (
                    summed
                    + bank[chosen, (2 * REACH + 1) * u + v]
                    * shifted[v, start : start + TILE_ROWS, :]
                )
        result[plane] = summed


def short_tables():
    index = np.arange(LANES)
    angle = 2.0 * np.pi * (index[:, None] * index[None, :] % LANES) / LANES
    cos, sin = np.cos(angle), np.sin(angle)
    table = np.block([[cos, -sin], [sin, cos]]).astype(np.float32)
    high = table.astype(BF16)
    low = (table - high.astype(np.float32)).astype(BF16)
    spin = 2.0 * np.pi * (np.arange(GROUPS)[:, None] * index[None, :]) / RANGE_BINS
    return high, low, np.cos(spin).astype(np.float32), np.sin(spin).astype(np.float32)


def shards(peers, swaths, *args):
    (polar, taps, weights, shifts, gains, owner, block_weights, kernel_index, bank) = args
    sections = taps.shape[0]
    vmem = pl.BlockSpec(memory_space=pltpu.VMEM)
    smem = pl.BlockSpec(memory_space=pltpu.SMEM)
    wide = pltpu.VMEM((ANGLES, GROUPS * WIDE), F32)
    tables = [jnp.asarray(t) for t in short_tables()]
    return pl.pallas_call(
        functools.partial(kernel, peers, swaths, sections),
        out_shape=jax.ShapeDtypeStruct((2, TILE_ROWS, LANES), F32),
        in_specs=[vmem] * 5 + [smem, vmem, smem, smem] + [vmem] * 4,
        out_specs=vmem,
        scratch_shapes=[
            pltpu.VMEM((GROUPS, TILE_ROWS, WIDE), F32),
            pltpu.VMEM((sections, 2, GROUPS, 2, ANGLES, LANES), F32),
            *([wide] * 9),
            pltpu.VMEM((ANGLES, ANGLES), F32),
            pltpu.VMEM((ANGLES, ANGLES), F32),
            pltpu.VMEM((2 * peers, TILE_ROWS, WIDE), F32),
            pltpu.VMEM((peers, TILE_ROWS, WIDE), F32),
            pltpu.VMEM((2, 3, EDGE, WIDE), F32),
            pltpu.VMEM((2, 2, EDGE, LANES), F32),
            pltpu.VMEM((2, LANES, TILE_ROWS), F32),
            pltpu.VMEM((2 * REACH + 1, TILE_ROWS + 2 * EDGE, LANES), F32),
            pltpu.SemaphoreType.DMA((sections, CHUNKS)),
            pltpu.SemaphoreType.DMA((sections, CHUNKS)),
            pltpu.SemaphoreType.DMA((2,)),
            pltpu.SemaphoreType.DMA((peers,)),
            pltpu.SemaphoreType.DMA((peers,)),
            pltpu.SemaphoreType.DMA((8,)),
            pltpu.SemaphoreType.DMA((8,)),
        ],
        compiler_params=pltpu.CompilerParams(
            collective_id=0, has_side_effects=True, vmem_limit_bytes=60 * 2**20
        ),
    )(
        polar,
        taps,
        weights,
        shifts,
        gains,
        owner.reshape(-1),
        block_weights,
        kernel_index.reshape(-1),
        bank,
        *tables,
    )


def solution(mesh):
    peers, swaths = mesh.shape["aper"], mesh.shape["swath"]
    in_specs = (
        P(None, "aper", "swath"),
        P(None, "aper", None, None, None),
        P(None, "aper", None, None, None),
        P(None, "aper", None, None),
        P(None, "swath"),
        P("aper", "swath", None, None),
        P("aper", "swath", None, None, None),
        P("aper", "swath"),
        P(),
    )
    return jax.shard_map(
        functools.partial(shards, peers, swaths),
        mesh=mesh,
        in_specs=in_specs,
        out_specs=P(None, "aper", "swath"),
        check_vma=False,
    )
```

profile of v0, /device:TPU:1, one launch (start us, length us, event | category | flops | bytes accessed | tf_op | source)
XLA Modules:
  0.0 67.0 jit_solution(234460447650707145)
XLA Ops:
  0.7 64.7 %shard_map.127 = f32[2,128,128]{2,1,0:T(8,128)} custom-call(f32[2,128,1024]{2,1,0:T(8,128)} %polar.1, s32[3,1,2,8,128]{4,3,2,1,0:T(8,128)} %taps.1, f32[3,1,2,8,128]{4,3,2,1,0:T(8,128)} %weights.1, f32[3,1,2,128]{3,2,1,0:T(2,128)} %shifts.1, f32[3,1024]{1,0:T(4,128)} %gains.1, s32[8]{0:T(128)} %bitcast.3, f32[1,1,8,128,128]{4,3,2,1,0:T(8,128)} %block_weights.1, ...), custom_call_target="tpu_custom_call" | custom-call | tf_op jit(solution)/shard_map/pallas_call | solution.py:457
  65.4 1.6 %copy.16 = f32[2,128,128]{2,1,0:T(8,128)} copy(f32[2,128,128]{2,1,0:T(8,128)} %shard_map.127) | data formatting | bytes 262144
where the time goes:
time: 67.2 us; the launch traced here: 67 us
  Pallas kernels  64.7 us (96%)
  local copies, waits for them, and re-layouts  1.57 us (2%)
    pallas_call x1, Pallas kernels, shards(): pl.pallas_call(functools.partial(kernel, peers, swaths, sections), out_sh...  64.7 us
    unnamed x1, local copies, waits for them, and re-layouts  1.57 us

commit v1 on v0

--- a/solution.py
+++ b/solution.py
@@ -16,8 +16,10 @@
 WIDE = 2 * LANES
 TILE_ROWS = 128
 TAPS = 8
-CHUNKS = 4
+CHUNKS = 16
+MIXES = 4
 ROWS = ANGLES // CHUNKS
+BLOCK = ANGLES // MIXES
 EDGE = 8
 REACH = 4
 MESH = pl.DeviceIdType.MESH
@@ -107,13 +109,13 @@
     peers,
     swaths,
     sections,
-    polar,
+    polar_in,
     taps,
     weights,
     shifts,
     gains,
     owner,
-    block_weights,
+    weights_in,
     kernel_index,
     bank,
     table_high,
@@ -121,6 +123,10 @@
     cos_ref,
     sin_ref,
     result,
+    polar,
+    block_weights,
+    weights_high,
+    weights_low,
     matrix,
     phases,
     spec0,
@@ -140,6 +146,7 @@
     col_halo,
     flipped,
     shifted,
+    in_sem,
     send_sem,
     recv_sem,
     mat_sem,
@@ -164,6 +171,18 @@
     for da, ds in around:
         where = (lax.rem(me + da + peers, peers), lax.rem(column + ds + swaths, swaths))
         pl.semaphore_signal(barrier, inc=1, device_id=where, device_id_type=MESH)
+
+    loads = [
+        pltpu.make_async_copy(
+            polar_in.at[:, pl.ds(k * BLOCK, BLOCK)],
+            polar.at[:, pl.ds(k * BLOCK, BLOCK)],
+            in_sem.at[k],
+        )
+        for k in range(MIXES)
+    ]
+    loads.append(pltpu.make_async_copy(weights_in.at[0, 0], block_weights, in_sem.at[MIXES]))
+    for load in loads:
+        load.start()
 
     bits = [lax.rem(me // (1 << step), 2) for step in range(levels)]
     table = (table_high[...], table_low[...])
@@ -205,6 +224,12 @@
     def chunk(k):
         return slice(k * ROWS, (k + 1) * ROWS)
 
+    def block(k):
+        return slice(k * BLOCK, (k + 1) * BLOCK)
+
+    def inside(k):
+        return range(k * CHUNKS // MIXES, (k + 1) * CHUNKS // MIXES)
+
     def exchange(step, k, source, target):
         return pltpu.make_async_remote_copy(
             src_ref=source.at[pl.ds(k * ROWS, ROWS)],
@@ -229,8 +254,9 @@
     everything = slice(0, ANGLES)
 
     copies0 = []
-    for k in range(CHUNKS):
-        rows = chunk(k)
+    for k in range(MIXES):
+        rows = block(k)
+        loads[k].wait()
         pairs = [
             (polar[0, rows, g * LANES : (g + 1) * LANES], polar[1, rows, g * LANES : (g + 1) * LANES])
             for g in range(GROUPS)
@@ -238,8 +264,9 @@
         store_wide(spec0, rows, forward(pairs, table, cos_ref, sin_ref))
         if k == 0:
             pl.semaphore_wait(barrier, levels + len(around))
-        copies0.append(exchange(0, k, spec0, got0))
-        copies0[-1].start()
+        for j in inside(k):
+            copies0.append(exchange(0, j, spec0, got0))
+            copies0[-1].start()
     mat_send[...] = interp(1, 1 - bits[1])
     mat_copy = pltpu.make_async_remote_copy(
         src_ref=mat_send,
@@ -253,8 +280,13 @@
     fill_phases(0, 0, bits[0])
     fill_phases(0, 1, 1 - bits[0])
 
+    def lefts_of(step):
+        return [split(interp(step, child)) for child in (bits[step], 1 - bits[step])]
+
+    lefts = {0: lefts_of(0)}
+
     def mix(step, side, source, first):
-        left = split(interp(step, bits[step] if side == 0 else 1 - bits[step]))
+        left = lefts[step][side]
         for group in range(GROUPS):
             value = product(left, split(source[:, lanes(group)]))
             value = steered(step, side, group, everything, value)
@@ -266,20 +298,22 @@
     for copy in copies0:
         copy.wait()
     mix(0, 1, got0, False)
-    for k in range(CHUNKS):
-        rows = chunk(k)
+    for k in range(MIXES):
+        rows = block(k)
         pairs = inverse(merged_rows(rows), table, cos_ref, sin_ref, gains[0:1, :])
         store_wide(spec1, rows, forward(pairs, table, cos_ref, sin_ref))
 
     mat_copy.wait()
     copies1 = []
-    for k in range(CHUNKS):
-        rows = chunk(k)
+    for k in range(MIXES):
+        rows = block(k)
         left = split(mat_got[rows, :])
         for group in range(GROUPS):
             mixed[rows, lanes(group)] = product(left, split(spec1[:, lanes(group)]))
-        copies1.append(exchange(1, k, mixed, got1))
-        copies1[-1].start()
+        for j in inside(k):
+            copies1.append(exchange(1, j, mixed, got1))
+            copies1[-1].start()
+    lefts[1] = lefts_of(1)
     fill_phases(1, 0, bits[1])
     fill_phases(1, 1, 1 - bits[1])
     mix(1, 0, spec1, True)
@@ -300,18 +334,22 @@
         if k == 0:
             fill_phases(2, 0, bits[2])
             fill_phases(2, 1, 1 - bits[2])
+            lefts[2] = lefts_of(2)
+            loads[MIXES].wait()
+            for q in range(GROUPS):
+                weights_high[q], weights_low[q] = split(block_weights[q])
 
     mix(2, 0, spec2, True)
     for copy in copies2:
         copy.wait()
     mix(2, 1, got2, False)
-    for k in range(CHUNKS):
-        rows = chunk(k)
+    for k in range(MIXES):
+        rows = block(k)
         pairs = inverse(merged_rows(rows), table, cos_ref, sin_ref, gains[2:3, :])
         store_wide(image, rows, [jnp.concatenate(pair, axis=1) for pair in pairs])
 
     for q in range(GROUPS):
-        matrix[q] = product(split(block_weights[0, 0, q]), split(image[:, lanes(q)]))
+        matrix[q] = product((weights_high[q], weights_low[q]), split(image[:, lanes(q)]))
 
     def gathered(d):
         value = None
@@ -320,13 +358,13 @@
             value = hit * matrix[q] if value is None else value + hit * matrix[q]
         return value
 
-    def part_copy(level, slot, source, target):
+    def part_copy(bit, half_at, slot, source, target):
         return pltpu.make_async_remote_copy(
             src_ref=source,
             dst_ref=target,
-            send_sem=part_send.at[slot],
-            recv_sem=part_recv.at[slot],
-            device_id=(me ^ (1 << level), column),
+            send_sem=part_send.at[half_at, slot],
+            recv_sem=part_recv.at[half_at, slot],
+            device_id=(me ^ (1 << bit), column),
             device_id_type=MESH,
         )
 
@@ -334,7 +372,7 @@
     copies = []
     for d in range(half):
         part[half + d] = gathered(2 * d + 1 - bits[0])
-        copies.append(part_copy(0, d, part.at[half + d], part_got.at[d]))
+        copies.append(part_copy(0, 0, d, part.at[half + d], part_got.at[d]))
         copies[-1].start()
     for d in range(half):
         part[d] = gathered(2 * d + bits[0])
@@ -343,23 +381,27 @@
         part[d] = part[d] + part_got[d]
     base, here = half, 0
     count = half
+    cuts = [pl.ds(h * (TILE_ROWS // 2), TILE_ROWS // 2) for h in range(2)]
     for level in range(1, levels):
         count = count // 2
         copies = []
-        for d in range(count):
-            copies.append(
-                part_copy(
-                    level,
-                    base + d,
-                    part.at[here + 2 * d + 1 - bits[level]],
-                    part_got.at[base + d],
+        for e in range(count):
+            for h, cut in enumerate(cuts):
+                bit = level if h == 0 else levels - level
+                away = 1 - bits[bit]
+                index = here + (2 * e + away if h == 0 else away * count + e)
+                copy = part_copy(
+                    bit, h, base + e, part.at[index, cut], part_got.at[base + e, cut]
                 )
-            )
-            copies[-1].start()
+                copy.start()
+                copies.append(copy)
         after = peers + base - half
-        for d in range(count):
-            copies[d].wait()
-            part[after + d] = part[here + 2 * d + bits[level]] + part_got[base + d]
+        for e in range(count):
+            for h, cut in enumerate(cuts):
+                bit = level if h == 0 else levels - level
+                index = here + (2 * e + bits[bit] if h == 0 else bits[bit] * count + e)
+                copies[2 * e + h].wait()
+                part[after + e, cut] = part[index, cut] + part_got[base + e, cut]
         here = after
         base = base + count
     tile = part.at[here]
@@ -452,14 +494,19 @@
     sections = taps.shape[0]
     vmem = pl.BlockSpec(memory_space=pltpu.VMEM)
     smem = pl.BlockSpec(memory_space=pltpu.SMEM)
+    anywhere = pl.BlockSpec(memory_space=pl.ANY)
     wide = pltpu.VMEM((ANGLES, GROUPS * WIDE), F32)
     tables = [jnp.asarray(t) for t in short_tables()]
     return pl.pallas_call(
         functools.partial(kernel, peers, swaths, sections),
         out_shape=jax.ShapeDtypeStruct((2, TILE_ROWS, LANES), F32),
-        in_specs=[vmem] * 5 + [smem, vmem, smem, smem] + [vmem] * 4,
+        in_specs=[anywhere] + [vmem] * 4 + [smem, anywhere, smem, smem] + [vmem] * 4,
         out_specs=vmem,
         scratch_shapes=[
+            pltpu.VMEM(polar.shape, F32),
+            pltpu.VMEM((GROUPS, TILE_ROWS, ANGLES), F32),
+            pltpu.VMEM((GROUPS, TILE_ROWS, ANGLES), BF16),
+            pltpu.VMEM((GROUPS, TILE_ROWS, ANGLES), BF16),
             pltpu.VMEM((GROUPS, TILE_ROWS, WIDE), F32),
             pltpu.VMEM((sections, 2, GROUPS, 2, ANGLES, LANES), F32),
             *([wide] * 9),
@@ -471,11 +518,12 @@
             pltpu.VMEM((2, 2, EDGE, LANES), F32),
             pltpu.VMEM((2, LANES, TILE_ROWS), F32),
             pltpu.VMEM((2 * REACH + 1, TILE_ROWS + 2 * EDGE, LANES), F32),
+            pltpu.SemaphoreType.DMA((MIXES + 1,)),
             pltpu.SemaphoreType.DMA((sections, CHUNKS)),
             pltpu.SemaphoreType.DMA((sections, CHUNKS)),
             pltpu.SemaphoreType.DMA((2,)),
-            pltpu.SemaphoreType.DMA((peers,)),
-            pltpu.SemaphoreType.DMA((peers,)),
+            pltpu.SemaphoreType.DMA((2, peers)),
+            pltpu.SemaphoreType.DMA((2, peers)),
             pltpu.SemaphoreType.DMA((8,)),
             pltpu.SemaphoreType.DMA((8,)),
         ],

time: 67.2 us -> 59.8 us (0.89)
  Pallas kernels: 64.7 us -> 57.4 us
    pallas_call x1, Pallas kernels: 64.7 us -> 57.4 us  [shards(): pl.pallas_call(functools.partial(kernel, peers, swaths, sections), out_sh...]
where the time goes in v1:
time: 59.8 us; the launch traced here: 59.6 us
  Pallas kernels  57.4 us (96%)
  local copies, waits for them, and re-layouts  1.57 us (3%)
  between operations  0.66 us (1%)
    pallas_call x1, Pallas kernels, shards(): pl.pallas_call(functools.partial(kernel, peers, swaths, sections), out_sh...  57.4 us
    unnamed x1, local copies, waits for them, and re-layouts  1.57 us

profile of v1, /device:TPU:1, one launch (start us, length us, event | category | flops | bytes accessed | tf_op | source)
XLA Modules:
  0.0 59.6 jit_solution(3327310460636504523)
XLA Ops:
  0.7 57.4 %shard_map.127 = f32[2,128,128]{2,1,0:T(8,128)} custom-call(f32[2,128,1024]{2,1,0:T(8,128)} %polar_in.1, s32[3,1,2,8,128]{4,3,2,1,0:T(8,128)} %taps.1, f32[3,1,2,8,128]{4,3,2,1,0:T(8,128)} %weights.1, f32[3,1,2,128]{3,2,1,0:T(2,128)} %shifts.1, f32[3,1024]{1,0:T(4,128)} %gains.1, s32[8]{0:T(128)} %bitcast.3, f32[1,1,8,128,128]{4,3,2,1,0:T(8,128)} %weights_in.1, ...), custom_call_target="tpu_custom_call" | custom-call | tf_op jit(solution)/shard_map/pallas_call | solution.py:500
  58.0 1.6 %copy.16 = f32[2,128,128]{2,1,0:T(8,128)} copy(f32[2,128,128]{2,1,0:T(8,128)} %shard_map.127) | data formatting | bytes 262144

commit v2 on v1

--- a/solution.py
+++ b/solution.py
@@ -253,6 +253,14 @@
 
     everything = slice(0, ANGLES)
 
+    fill_phases(0, 0, bits[0])
+    fill_phases(0, 1, 1 - bits[0])
+    mat_send[...] = interp(1, 1 - bits[1])
+
+    def lefts_of(step):
+        return [split(interp(step, child)) for child in (bits[step], 1 - bits[step])]
+
+    lefts = {0: lefts_of(0)}
     copies0 = []
     for k in range(MIXES):
         rows = block(k)
@@ -267,7 +275,6 @@
         for j in inside(k):
             copies0.append(exchange(0, j, spec0, got0))
             copies0[-1].start()
-    mat_send[...] = interp(1, 1 - bits[1])
     mat_copy = pltpu.make_async_remote_copy(
         src_ref=mat_send,
         dst_ref=mat_got,
@@ -277,13 +284,6 @@
         device_id_type=MESH,
     )
     mat_copy.start()
-    fill_phases(0, 0, bits[0])
-    fill_phases(0, 1, 1 - bits[0])
-
-    def lefts_of(step):
-        return [split(interp(step, child)) for child in (bits[step], 1 - bits[step])]
-
-    lefts = {0: lefts_of(0)}
 
     def mix(step, side, source, first):
         left = lefts[step][side]

time: 59.8 us -> 59.7 us (level)
  no operation moved by 1% of the time
where the time goes in v2:
time: 59.7 us; the launch traced here: 59.5 us
  Pallas kernels  57.3 us (96%)
  local copies, waits for them, and re-layouts  1.57 us (3%)
  between operations  0.66 us (1%)
    pallas_call x1, Pallas kernels, shards(): pl.pallas_call(functools.partial(kernel, peers, swaths, sections), out_sh...  57.3 us
    unnamed x1, local copies, waits for them, and re-layouts  1.57 us

profile of v2, /device:TPU:1, one launch (start us, length us, event | category | flops | bytes accessed | tf_op | source)
XLA Modules:
  0.0 59.5 jit_solution(12236333500830185705)
XLA Ops:
  0.7 57.3 %shard_map.127 = f32[2,128,128]{2,1,0:T(8,128)} custom-call(f32[2,128,1024]{2,1,0:T(8,128)} %polar_in.1, s32[3,1,2,8,128]{4,3,2,1,0:T(8,128)} %taps.1, f32[3,1,2,8,128]{4,3,2,1,0:T(8,128)} %weights.1, f32[3,1,2,128]{3,2,1,0:T(2,128)} %shifts.1, f32[3,1024]{1,0:T(4,128)} %gains.1, s32[8]{0:T(128)} %bitcast.3, f32[1,1,8,128,128]{4,3,2,1,0:T(8,128)} %weights_in.1, ...), custom_call_target="tpu_custom_call" | custom-call | tf_op jit(solution)/shard_map/pallas_call | solution.py:500
  58.0 1.6 %copy.16 = f32[2,128,128]{2,1,0:T(8,128)} copy(f32[2,128,128]{2,1,0:T(8,128)} %shard_map.127) | data formatting | bytes 262144
